TPU v7x, 32 devices: a whole 2x2x4 slice. The times are simulated.
32 devices in a mesh: group: 4 (over x, core), seq: 8 (over z, y).
Axes of the slice: x: 2, y: 2, z: 4, core: 2. Of those that a mesh axis runs over, the one named last changes fastest.
Arguments:
- features: bfloat16 [16, 64, 16, 384], P('group', 'seq'), parts along dimension 0, may hold values from -6 to 6
- cotangent: bfloat16 [16, 64, 16, 192], P('group', 'seq'), parts along dimension 0, may hold values from -6 to 6
- conv_weight: bfloat16 [3, 3, 3, 384, 192], replicated, may hold values from -0.0625 to 0.0625
- patch_map: bfloat16 [1536, 4096], P('seq'), may hold values from -0.15625 to 0.15625
- qkv: bfloat16 [3, 4096, 4096], P(None, ('group', 'seq')), parts along dimension 1, may hold values from -122 to 122
Outputs:
- weight_grad: float32 [12, 3, 3, 384, 192], P('group'), parts along dimension 0
- grad_qkv: bfloat16 [3, 4096, 4096], P(None, ('group', 'seq')), parts along dimension 1
There are 4 independent parts, one for each index of `group`. A program takes and returns all parts, laid end to end along the dimension named above; an argument that names none is the same for every part. Nothing has to cross between parts.
All inputs are finite; a program needn't handle non-finite values.
Results may differ from a plain program's by a relative error of at most 0.0075.
Values may be sent and summed in bfloat16 or wider, within the bound.
A program may use at most 128 MiB of HBM per device.

v0:
```python
import math

import jax
import jax.numpy as jnp
from jax import lax
from jax.sharding import PartitionSpec as P

HEADS = 32


def extended(cells, sides, width):
    for axis, dim in sides:
        count = lax.axis_size(axis)
        ends = count - 1
        head = lax.slice_in_dim(cells, 0, width, axis=dim)
        tail = lax.slice_in_dim(cells, cells.shape[dim] - width, cells.shape[dim], axis=dim)
        cells = jnp.concatenate(
            [
                lax.ppermute(tail, axis, [(i, (i + 1) % count) for i in range(ends)]),
                cells,
                lax.ppermute(head, axis, [((i + 1) % count, i) for i in range(ends)]),
            ],
            axis=dim,
        )
    return cells


def attend_head(query, keys, values, grad_out):
    length, width = query.shape
    scale = 1.0 / math.sqrt(width)
    block = min(512, length)
    count = length // block

    def step(carry, index):
        acc_keys, acc_values = carry
        start = index * block
        query_rows = lax.dynamic_slice_in_dim(query, start, block, 0)
        grad_rows = lax.dynamic_slice_in_dim(grad_out, start, block, 0)
        scores = (
            lax.dot_general(
                query_rows, keys, (((1,), (1,)), ((), ())), preferred_element_type=jnp.float32
            )
            * scale
        )
        top = jnp.max(scores, axis=1, keepdims=True)
        expo = jnp.exp(scores - top)
        probs = expo / jnp.sum(expo, axis=1, keepdims=True)
        dprob = lax.dot_general(
            grad_rows, values, (((1,), (1,)), ((), ())), preferred_element_type=jnp.float32
        )
        delta = jnp.sum(probs * dprob, axis=1, keepdims=True)
        dscore = (probs * (dprob - delta) * scale).astype(jnp.bfloat16)
        pround = probs.astype(jnp.bfloat16)
        dquery = jnp.dot(dscore, keys, preferred_element_type=jnp.float32).astype(jnp.bfloat16)
        acc_keys = acc_keys + lax.dot_general(
            dscore, query_rows, (((0,), (0,)), ((), ())), preferred_element_type=jnp.float32
        )
        acc_values = acc_values + lax.dot_general(
            pround, grad_rows, (((0,), (0,)), ((), ())), preferred_element_type=jnp.float32
        )
        return ((acc_keys, acc_values), dquery)

    zeros_init = jnp.zeros((length, width), jnp.float32)
    (acc_keys, acc_values), dquery = lax.scan(step, (zeros_init, zeros_init), jnp.arange(count))
    return (
        dquery.reshape(length, width),
        acc_keys.astype(jnp.bfloat16),
        acc_values.astype(jnp.bfloat16),
    )


def per_device(features, cotangent, conv_weight, patch_map, qkv):
    frames, rows_here, cols, cin = features.shape
    cout = cotangent.shape[3]
    devices_seq = lax.axis_size("seq")
    padded = extended(cotangent, (("seq", 1),), 1)
    padded = jnp.pad(padded, ((0, 2), (0, 0), (1, 1), (0, 0)))
    flat_in = features.reshape(-1, cin)
    grad_in = jnp.zeros((frames * rows_here * cols, cin), jnp.float32)
    taps = []
    for tap_t in range(3):
        for tap_h in range(3):
            for tap_w in range(3):
                shifted = padded[
                    2 - tap_t : 2 - tap_t + frames,
                    2 - tap_h : 2 - tap_h + rows_here,
                    2 - tap_w : 2 - tap_w + cols,
                ]
                shifted = shifted.reshape(-1, cout)
                grad_in = grad_in + lax.dot_general(
                    shifted,
                    conv_weight[tap_t, tap_h, tap_w],
                    (((1,), (1,)), ((), ())),
                    preferred_element_type=jnp.float32,
                )
                taps.append(
                    lax.dot_general(
                        flat_in,
                        shifted,
                        (((0,), (0,)), ((), ())),
                        preferred_element_type=jnp.float32,
                    )
                )
    local_grad = jnp.stack(taps).reshape(3, 3, 3, cin, cout)
    weight_grad = lax.psum(local_grad, "seq") * (
        1.0 / math.sqrt(frames * rows_here * devices_seq * cols)
    )
    grad_in = grad_in.reshape(frames, rows_here // 2, 2, cols // 2, 2, cin).transpose(
        1, 0, 3, 2, 4, 5
    )
    patches = grad_in.reshape(-1, 4 * cin).astype(jnp.bfloat16)
    tokens_here = patches.shape[0]
    inner = qkv.shape[2]
    heads_n = HEADS
    head_dim = inner // heads_n
    stacked = qkv.reshape(3, tokens_here, heads_n, head_dim)
    grad_out = jnp.dot(
        patches,
        lax.all_gather(patch_map, "seq", axis=0, tiled=True),
        preferred_element_type=jnp.float32,
    ).astype(jnp.bfloat16)
    grad_four = grad_out.reshape(1, tokens_here, heads_n, head_dim)
    moved, moved_grad = (
        lax.all_to_all(stacked, "seq", split_axis=2, concat_axis=1, tiled=True),
        lax.all_to_all(grad_four, "seq", split_axis=2, concat_axis=1, tiled=True),
    )
    head_grad = moved_grad[0]
    moved = moved.transpose(0, 2, 1, 3)
    head_grad = head_grad.transpose(1, 0, 2)

    def one_head(packed):
        return attend_head(packed[0], packed[1], packed[2], packed[3])

    dquery, dkeys, dvalues = lax.map(one_head, (moved[0], moved[1], moved[2], head_grad))
    result = jnp.stack([dquery, dkeys, dvalues]).transpose(0, 2, 1, 3)
    back = lax.all_to_all(result, "seq", split_axis=1, concat_axis=2, tiled=True)
    return (weight_grad, back.reshape(3, tokens_here, inner))


def solution(mesh):
    placed = (
        P("group", "seq", None, None),
        P("group", "seq", None, None),
        P(),
        P("seq", None),
        P(None, ("group", "seq"), None),
    )
    return jax.shard_map(
        per_device,
        mesh=mesh,
        in_specs=placed,
        out_specs=(P("group", None, None, None, None), P(None, ("group", "seq"), None)),
        check_vma=False,
    )
```

profile of v0, /device:TPU:0, one launch (start us, length us, event | category | flops | bytes accessed | tf_op | source)
XLA Modules:
  0.0 613.0 jit_solution(14753593938008118117)
XLA Ops:
  9.3 5.5 collective-permute-start
  16.1 3.5 copy.18
  21.5 7.2 %all-to-all-start = ((bf16[3,128,32,128]{1,3,0,2:T(8,128)(2,1)}), bf16[3,128,32,128]{1,3,0,2:T(8,128)(2,1)}, u32[]{:S(2)}, u32[]{:S(2)}) async-start(bf16[3,128,32,128]{1,3,0,2:T(8,128)(2,1)} %copy.19), calls=%async_computation | async-start | bytes 6291456 | tf_op jit(solution)/shard_map/all_to_all | solution.py:124
  61.4 185.2 %all-gather.2.cloned.1.call-done = bf16[1536,4096]{1,0:T(8,128)(2,1)} async-done(((bf16[192,4096]{1,0:T(8,128)(2,1)}), bf16[1536,4096]{1,0:T(8,128)(2,1)}) %all-gather.2.cloned.1.call-update) | async-done | bytes 12582928 | tf_op jit(solution)/shard_map/all_gather | solution.py:119
  246.6 6.6 %fusion.21 = bf16[16,8,32,128]{3,1,2,0:T(8,128)(2,1)S(1)} fusion(bf16[128,1536]{1,0:T(8,128)(2,1)S(1)} %convert_element_type.35, bf16[1536,4096]{1,0:T(8,128)(2,1)} %all-gather.2.cloned.1.call-done), kind=kOutput, calls=%fused_computation.40 | convolution fusion | flops 1611137024 | bytes 14024704 | tf_op jit(solution)/shard_map/dot_general | solution.py:117
  254.9 4.2 all-to-all-start.1
  266.3 3.5 copy.21
  271.5 30.2 %all-to-all-done.1 = bf16[1,128,32,128]{3,1,0,2:T(8,128)(2,1)} async-done(((bf16[1,128,32,128]{3,1,0,2:T(8,128)(2,1)}), bf16[1,128,32,128]{3,1,0,2:T(8,128)(2,1)}, u32[]{:S(2)}, u32[]{:S(2)}) %all-to-all-start.1) | async-done | bytes 1048608 | tf_op jit(solution)/shard_map/all_to_all | solution.py:125
  304.0 96.7 %while.30 = (s32[]{:T(128)}, bf16[4,1024,128]{2,1,0:T(8,128)(2,1)}, bf16[4,1024,128]{2,1,0:T(8,128)(2,1)}, bf16[4,1024,128]{2,1,0:T(8,128)(2,1)}, bf16[4,1024,12...) while((s32[]{:T(128)}, bf16[4,1024,128]{2,1,0:T(8,128)(2,1)}, ...), condition=%wide.region_7.8_spmd, body=%wide.region_1.7_spmd.sunk | while | flops 682949120 | bytes 26632184 | solution.py:134
  308.7 15.9 %while.31 = (s32[]{:T(128)}, f32[1024,128]{1,0:T(8,128)S(1)}, f32[1024,128]{1,0:T(8,128)}, bf16[2,512,128]{2,1,0:T(8,128)(2,1)}, s32[2]{0:T(128)S(1)}, /*index=5...) while((s32[]{:T(128)}, f32[1024,128]{1,0:T(8,128)S(1)}, ...), condition=%wide.region_6.6_spmd.clone, body=%wide.region_2.5_spmd.clone.sunk | while | flops 682686976 | bytes 22436588 | solution.py:64
  318.5 2.6 convolution_add_fusion.30
  332.8 15.9 %while.31 = (s32[]{:T(128)}, f32[1024,128]{1,0:T(8,128)S(1)}, f32[1024,128]{1,0:T(8,128)}, bf16[2,512,128]{2,1,0:T(8,128)(2,1)}, s32[2]{0:T(128)S(1)}, /*index=5...) while((s32[]{:T(128)}, f32[1024,128]{1,0:T(8,128)S(1)}, ...), condition=%wide.region_6.6_spmd.clone, body=%wide.region_2.5_spmd.clone.sunk | while | flops 682686976 | bytes 22436588 | solution.py:64
  342.7 2.6 convolution_add_fusion.30
  357.0 15.9 %while.31 = (s32[]{:T(128)}, f32[1024,128]{1,0:T(8,128)S(1)}, f32[1024,128]{1,0:T(8,128)}, bf16[2,512,128]{2,1,0:T(8,128)(2,1)}, s32[2]{0:T(128)S(1)}, /*index=5...) while((s32[]{:T(128)}, f32[1024,128]{1,0:T(8,128)S(1)}, ...), condition=%wide.region_6.6_spmd.clone, body=%wide.region_2.5_spmd.clone.sunk | while | flops 682686976 | bytes 22436588 | solution.py:64
  366.8 2.6 convolution_add_fusion.30
  381.2 15.9 %while.31 = (s32[]{:T(128)}, f32[1024,128]{1,0:T(8,128)S(1)}, f32[1024,128]{1,0:T(8,128)}, bf16[2,512,128]{2,1,0:T(8,128)(2,1)}, s32[2]{0:T(128)S(1)}, /*index=5...) while((s32[]{:T(128)}, f32[1024,128]{1,0:T(8,128)S(1)}, ...), condition=%wide.region_6.6_spmd.clone, body=%wide.region_2.5_spmd.clone.sunk | while | flops 682686976 | bytes 22436588 | solution.py:64
  391.1 2.6 convolution_add_fusion.30
  402.8 3.2 copy_bitcast_fusion
  406.0 3.6 maximum_bitcast_fusion
  409.6 4.5 all-to-all-start.2
  414.0 175.9 %all-reduce.3.cloned.1.call-done = f32[3,3,3,384,192]{3,4,2,1,0:T(8,128)} async-done(((f32[3,3,3,384,192]{3,4,2,1,0:T(8,128)}), f32[3,3,3,384,192]{3,4,2,1,0:T(8,128)}) %all-reduce.3.cloned.1.call-update) | async-done | bytes 7962640 | tf_op jit(solution)/shard_map/psum | solution.py:105
  589.9 7.4 %broadcast_multiply_fusion = f32[3,3,3,384,192]{3,4,2,1,0:T(8,128)} fusion(f32[3,3,3,384,192]{3,4,2,1,0:T(8,128)} %all-reduce.3.cloned.1.call-done), kind=kLoop, calls=%fused_computation.30 | loop fusion | flops 1990656 | bytes 15925248 | tf_op jit(solution)/shard_map/mul | solution.py:105
  597.3 2.8 copy.28
  600.1 6.1 reshape.141
  (208 shorter events, 132.7 us)
Async XLA Ops:
  7.2 33.4 %copy-start = (bf16[4,8,16,384]{3,2,1,0:T(8,128)(2,1)S(1)}, bf16[4,8,16,384]{3,2,1,0:T(8,128)(2,1)}, u32[]{:S(2)}) copy-start(bf16[4,8,16,384]{3,2,1,0:T(8,128)(2,1)} %param.9) | copy-start | bytes 1179652
  7.2 239.5 %all-gather.2.cloned.1.call-start = ((), (), s32[]{:S(2)}) async-start(), calls=%async_computation.4 | async-start | bytes 14155776 | tf_op jit(solution)/shard_map/all_gather | solution.py:119
  9.3 19.4 %collective-permute-start = (bf16[4,1,16,192]{3,2,1,0:T(8,128)(2,1)}, bf16[4,1,16,192]{3,2,1,0:T(8,128)(2,1)}, u32[]{:S(2)}, u32[]{:S(2)}) collective-permute-start(bf16[4,1,16,192]{3,2,1,0:T(8,128)(2,1)} %get-tuple-element.197), channel_id=1, source_target_pairs={{0,1},{1,2},{2,3},{3,4},{4,5},{5,6},{6,7},{8,9},{9,10},{10,11},{11... | collective-permute-start | bytes 73736 | tf_op jit(solution)/shard_map/ppermute | solution.py:19
  14.8 14.9 %collective-permute-start.1 = (bf16[4,1,16,192]{3,2,1,0:T(8,128)(2,1)}, bf16[4,1,16,192]{3,2,1,0:T(8,128)(2,1)}, u32[]{:S(2)}, u32[]{:S(2)}) collective-permute-start(bf16[4,1,16,192]{3,2,1,0:T(8,128)(2,1)} %get-tuple-element.198), channel_id=1, source_target_pairs={{1,0},{2,1},{3,2},{4,3},{5,4},{6,5},{7,6},{9,8},{10,9},{11,10},{12... | collective-permute-start | bytes 73736 | tf_op jit(solution)/shard_map/ppermute | solution.py:21
  21.5 8.2 %copy-start.3 = (bf16[4,8,16,192]{3,2,1,0:T(8,128)(2,1)S(1)}, bf16[4,8,16,192]{3,2,1,0:T(8,128)(2,1)}, u32[]{:S(2)}) copy-start(bf16[4,8,16,192]{3,2,1,0:T(8,128)(2,1)} %param.10) | copy-start | bytes 589828
  21.5 233.4 %all-to-all-start = ((bf16[3,128,32,128]{1,3,0,2:T(8,128)(2,1)}), bf16[3,128,32,128]{1,3,0,2:T(8,128)(2,1)}, u32[]{:S(2)}, u32[]{:S(2)}) async-start(bf16[3,128,32,128]{1,3,0,2:T(8,128)(2,1)} %copy.19), calls=%async_computation | async-start | bytes 6291456 | tf_op jit(solution)/shard_map/all_to_all | solution.py:124
  28.7 3.2 copy-start.4
  254.9 46.8 %all-to-all-start.1 = ((bf16[1,128,32,128]{3,1,0,2:T(8,128)(2,1)}), bf16[1,128,32,128]{3,1,0,2:T(8,128)(2,1)}, u32[]{:S(2)}, u32[]{:S(2)}) async-start(bf16[1,128,32,128]{3,1,0,2:T(8,128)(2,1)} %copy.23), calls=%async_computation.1 | async-start | bytes 2097152 | tf_op jit(solution)/shard_map/all_to_all | solution.py:125
  259.1 330.8 %all-reduce.3.cloned.1.call-start = ((), (), s32[]{:S(2)}) async-start(), calls=%async_computation.3 | async-start | bytes 15925248 | tf_op jit(solution)/shard_map/psum | solution.py:105
  311.1 1.6 copy-start.2
  318.5 2.6 copy-start.2
  335.2 1.6 copy-start.2
  342.6 2.6 copy-start.2
  359.4 1.6 copy-start.2
  366.8 2.6 copy-start.2
  383.6 1.6 copy-start.2
  391.0 2.6 copy-start.2
  409.6 187.7 %all-to-all-start.2 = ((bf16[3,1024,4,128]{3,2,0,1:T(4,128)(2,1)}), bf16[3,1024,4,128]{3,2,0,1:T(4,128)(2,1)S(1)}, u32[]{:S(2)}, u32[]{:S(2)}) async-start(bf16[3,1024,4,128]{3,2,0,1:T(4,128)(2,1)} %maximum_bitcast_fusion), calls=%async_computation.2 | async-start | bytes 6291456 | tf_op jit(solution)/shard_map/all_to_all | solution.py:136
  597.3 8.9 %copy-start.1 = (bf16[4,8,16,384]{3,2,1,0:T(8,128)(2,1)S(1)}, bf16[4,8,16,384]{3,2,1,0:T(8,128)(2,1)}, u32[]{:S(2)}) copy-start(bf16[4,8,16,384]{3,2,1,0:T(8,128)(2,1)} %param.9) | copy-start | bytes 1179652
Sparse Core Ops, SparseCore 0:
  10.2 236.4 all-gather.1
  266.4 323.4 all-reduce.2
where the time goes:
time: 615 us; the launch traced here: 613 us
  waiting for transfers between devices  392 us (64%)
  matrix products  84.4 us (14%)
  local copies, waits for them, and re-layouts  64.1 us (10%)
  other arithmetic  29.3 us (5%)
  starting transfers between devices  22.8 us (4%)
  between operations  14.4 us (2%)
    all_gather x1, waiting for transfers between devices, per_device(): lax.all_gather(patch_map, 'seq', axis=0, tiled=True)  185 us
    psum x1, waiting for transfers between devices, per_device(): lax.psum(local_grad, 'seq')  176 us
    all_to_all x1, waiting for transfers between devices, per_device(): lax.all_to_all(grad_four, 'seq', split_axis=2, concat_axis=1, tiled=True)  30.2 us
    dot_general x27, matrix products, per_device(): lax.dot_general(flat_in, shifted, (((0,), (0,)), ((), ())), preferred_ele...  27.2 us
    squeeze x16, local copies, waits for them, and re-layouts, per_device(): lax.map(one_head, (moved[0], moved[1], moved[2], head_grad))  18.5 us
    dot_general x8, matrix products, step(): lax.dot_general(pround, grad_rows, (((0,), (0,)), ((), ())), preferred_el...  16.7 us
  transfers between devices with their start and end apart: 7, of which 3 were waited for; matrix products, arithmetic and copies ran while one was open for 28% of the time, Pallas kernels for 0%

commit v1 on v0

v1 whole, which is shorter than its diff:
```python
import math

import jax
import jax.numpy as jnp
from jax import lax
from jax.experimental import pallas as pl
from jax.experimental.pallas import tpu as pltpu
from jax.sharding import PartitionSpec as P

HEADS = 32
TILE = 32
LIMIT = 60 * 1024 * 1024


def flops(count, moved):
    return pl.CostEstimate(flops=count, bytes_accessed=moved, transcendentals=0)


def grad_out_kernel(x_ref, w_ref, map_ref, out_ref, acc_ref):
    frames, span, wide = x_ref.shape[1], x_ref.shape[2], x_ref.shape[3]
    double = w_ref.shape[2]
    tap_h = pl.program_id(1)

    for side in range(2):
        for tap_t in (2, 1, 0):
            live = frames - 2 + tap_t
            rows = x_ref[side + 2 - tap_h, 2 - tap_t :].reshape(live * span, wide)
            part = lax.dot_general(
                rows, w_ref[tap_t, 0], (((1,), (1,)), ((), ())), preferred_element_type=jnp.float32
            )
            if tap_t == 2:

                @pl.when(tap_h == 0)
                def _():
                    acc_ref[side] = part

                @pl.when(tap_h > 0)
                def _():
                    acc_ref[side] += part

            else:
                acc_ref[side, : live * span] += part

    @pl.when(tap_h == 2)
    def _():
        wide_out = out_ref.shape[1]
        total = jnp.dot(
            acc_ref[0].astype(jnp.bfloat16), map_ref[:double], preferred_element_type=jnp.float32
        ) + jnp.dot(
            acc_ref[1].astype(jnp.bfloat16), map_ref[double:], preferred_element_type=jnp.float32
        )
        each = span // TILE
        total = total.reshape(frames, TILE, each, wide_out).transpose(1, 0, 2, 3)
        out_ref[...] = total.reshape(frames * span, wide_out).astype(jnp.bfloat16)


def weight_kernel(scale, blocks, feat_ref, x_ref, out_ref, turned_ref):
    frames, span, wide = x_ref.shape[1], x_ref.shape[2], x_ref.shape[3]
    double = feat_ref.shape[4]
    cin, cout = double // 2, wide // 4
    tap_h = pl.program_id(0)
    block = pl.program_id(1)

    def turn():
        for side in range(2):
            for frame in range(frames):
                turned_ref[side, :, frame * span : (frame + 1) * span] = (
                    feat_ref[:, side, frame].reshape(span, double).T
                )

    if blocks == 1:
        pl.when(tap_h == 0)(turn)
    else:
        turn()
    for tap_t in range(3):
        live = frames - 2 + tap_t
        prod = None
        for side in range(2):
            rows = x_ref[side + 2 - tap_h, 2 - tap_t :].reshape(live * span, wide)
            part = jnp.dot(
                turned_ref[side, :, : live * span], rows, preferred_element_type=jnp.float32
            )
            prod = part if prod is None else prod + part
        for tap_w in range(3):
            even = prod[:cin, cout * (2 - tap_w) : cout * (3 - tap_w)]
            odd = prod[cin:, cout * (3 - tap_w) : cout * (4 - tap_w)]
            value = (even + odd) * scale
            if blocks == 1:
                out_ref[tap_t, 0, tap_w] = value
            else:

                @pl.when(block == 0)
                def _():
                    out_ref[tap_t, 0, tap_w] = value

                @pl.when(block > 0)
                def _():
                    out_ref[tap_t, 0, tap_w] += value


def attention_kernel(step, qkv_ref, grad_ref, out_ref, dk_ref, dv_ref):
    shards, _, rows, width = qkv_ref.shape
    length = shards * rows
    scale = 1.0 / math.sqrt(width)
    keys = qkv_ref[:, 1].reshape(length, width)
    values = qkv_ref[:, 2].reshape(length, width)
    keys_t = keys.T
    span = step * rows

    def block(index, first):
        query = qkv_ref[pl.ds(index * step, step), 0].reshape(span, width)
        grads = grad_ref[pl.ds(pl.multiple_of(index * span, span), span), :]
        scores = lax.dot_general(
            keys, query, (((1,), (1,)), ((), ())), preferred_element_type=jnp.float32
        )
        top = jnp.max(scores, axis=0, keepdims=True)
        expo = jnp.exp((scores - top) * scale)
        probs = expo * (1.0 / jnp.sum(expo, axis=0, keepdims=True))
        dprob = lax.dot_general(
            values, grads, (((1,), (1,)), ((), ())), preferred_element_type=jnp.float32
        )
        delta = jnp.sum(probs * dprob, axis=0, keepdims=True)
        dscore = (probs * (dprob - delta)).astype(jnp.bfloat16)
        dquery = jnp.dot(keys_t, dscore, preferred_element_type=jnp.float32) * scale
        out_ref[pl.ds(index * step, step), 0] = (
            dquery.T.reshape(step, rows, width).astype(jnp.bfloat16)
        )
        part_k = jnp.dot(dscore, query, preferred_element_type=jnp.float32)
        part_v = jnp.dot(probs.astype(jnp.bfloat16), grads, preferred_element_type=jnp.float32)
        if first:
            dk_ref[...] = part_k
            dv_ref[...] = part_v
        else:
            dk_ref[...] += part_k
            dv_ref[...] += part_v

    count = shards // step
    if count <= 4:
        for index in range(count):
            block(index, index == 0)
    else:
        block(0, True)

        @pl.loop(1, count)
        def _(index):
            block(index, False)

    out_ref[:, 1] = (dk_ref[...] * scale).reshape(shards, rows, width).astype(jnp.bfloat16)
    out_ref[:, 2] = dv_ref[...].reshape(shards, rows, width).astype(jnp.bfloat16)


def per_device(features, cotangent, conv_weight, patch_map, qkv):
    frames, rows_here, cols, cin = features.shape
    cout = cotangent.shape[3]
    count = lax.axis_size("seq")
    parts = lax.axis_size("group")
    half, pairs = cols // 2, rows_here // 2
    pairs_all = pairs * count
    tokens_here, inner = qkv.shape[1], qkv.shape[2]
    length = tokens_here * count
    mine = inner // count
    head_dim = inner // HEADS

    cot = cotangent.reshape(frames, pairs, 2, half, 2 * cout).transpose(2, 0, 1, 3, 4)
    cot = lax.all_gather(cot.reshape(-1, 2 * cout), "seq", axis=0, tiled=True)
    sent = qkv.reshape(3, tokens_here, count, mine).transpose(2, 0, 1, 3)
    moved = lax.all_to_all(sent, "seq", split_axis=0, concat_axis=0, tiled=True)
    share = mine // parts
    depth = patch_map.shape[0]
    member = lax.axis_index("group")
    piece = lax.dynamic_index_in_dim(
        patch_map.reshape(depth, count, parts, share), member, axis=2, keepdims=False
    )
    piece = lax.all_to_all(
        piece.transpose(1, 0, 2), "seq", split_axis=0, concat_axis=0, tiled=True
    ).reshape(count * depth, share)
    columns = lax.all_gather(piece, "group", axis=0, tiled=False)
    columns = columns.transpose(1, 0, 2).reshape(count * depth, mine)
    feat = features.reshape(frames, pairs, 2, half, 2 * cin).transpose(2, 0, 1, 3, 4)
    feat = lax.all_gather(feat.reshape(-1, 2 * cin), "seq", axis=0, tiled=True)
    feat = feat.reshape(count, 2, frames, pairs * half, 2 * cin)

    full = cot.reshape(count, 2, frames, pairs, half, 2 * cout).transpose(1, 2, 0, 3, 4, 5)
    full = full.reshape(2, frames, pairs_all, half, 2 * cout)
    left = jnp.pad(full[:, :, :, :-1, cout:], ((0, 0), (0, 0), (0, 0), (1, 0), (0, 0)))
    right = jnp.pad(full[:, :, :, 1:, :cout], ((0, 0), (0, 0), (0, 0), (0, 1), (0, 0)))
    wide = jnp.concatenate([left, full, right], axis=-1)
    above = jnp.pad(wide[1][:, :-1], ((0, 0), (1, 0), (0, 0), (0, 0)))
    below = jnp.pad(wide[0][:, 1:], ((0, 0), (0, 1), (0, 0), (0, 0)))
    shifts = jnp.stack([above, wide[0], wide[1], below])
    shifts = shifts.reshape(4, frames, pairs_all * half, 4 * cout)

    taps = [conv_weight[:, :, tap_w] for tap_w in range(3)]
    blank = jnp.zeros_like(taps[0])
    big = jnp.concatenate(
        [
            jnp.concatenate([taps[2], taps[1], taps[0], blank], axis=-1),
            jnp.concatenate([blank, taps[2], taps[1], taps[0]], axis=-1),
        ],
        axis=2,
    )

    blocks = pairs_all // TILE
    span = TILE * half
    work = 2 * 9 * 3 * 2 * pairs_all * half * (2 * cin) * (4 * cout)
    x_block = pl.BlockSpec((4, frames, span, 4 * cout), lambda blk, tap: (0, 0, blk, 0))
    grad_out = pl.pallas_call(
        grad_out_kernel,
        grid=(blocks, 3),
        in_specs=[
            x_block,
            pl.BlockSpec((3, 1, 2 * cin, 4 * cout), lambda blk, tap: (0, tap, 0, 0)),
            pl.BlockSpec((count * depth, mine), lambda blk, tap: (0, 0)),
        ],
        out_specs=pl.BlockSpec((frames * span, mine), lambda blk, tap: (blk, 0)),
        out_shape=jax.ShapeDtypeStruct((length, mine), jnp.bfloat16),
        scratch_shapes=[pltpu.VMEM((2, frames * span, 2 * cin), jnp.float32)],
        compiler_params=pltpu.CompilerParams(vmem_limit_bytes=LIMIT),
        cost_estimate=flops(work, 20 << 20),
        name="grad_out",
    )(shifts, big, columns)

    step = max(1, 256 // tokens_here)
    head_block = pl.BlockSpec((count, 3, tokens_here, head_dim), lambda head: (0, 0, 0, head))
    heads_here = HEADS // count
    result = pl.pallas_call(
        lambda *refs: attention_kernel(step, *refs),
        grid=(heads_here,),
        in_specs=[head_block, pl.BlockSpec((length, head_dim), lambda head: (0, head))],
        out_specs=head_block,
        out_shape=jax.ShapeDtypeStruct((count, 3, tokens_here, mine), jnp.bfloat16),
        scratch_shapes=[pltpu.VMEM((length, head_dim), jnp.float32)] * 2,
        compiler_params=pltpu.CompilerParams(vmem_limit_bytes=LIMIT),
        cost_estimate=flops(heads_here * 20 * length * length * head_dim, 8 << 20),
        name="attention",
    )(moved, grad_out)

    shifts, result = lax.optimization_barrier((shifts, result))
    back = lax.all_to_all(result, "seq", split_axis=0, concat_axis=0, tiled=True)

    scale = 1.0 / math.sqrt(frames * rows_here * count * cols)
    shards = TILE // pairs
    weight_grad = pl.pallas_call(
        lambda *refs: weight_kernel(scale, blocks, *refs),
        grid=(3, blocks),
        in_specs=[
            pl.BlockSpec(
                (shards, 2, frames, pairs * half, 2 * cin), lambda tap, blk: (blk, 0, 0, 0, 0)
            ),
            pl.BlockSpec((4, frames, span, 4 * cout), lambda tap, blk: (0, 0, blk, 0)),
        ],
        out_specs=pl.BlockSpec((3, 1, 3, cin, cout), lambda tap, blk: (0, tap, 0, 0, 0)),
        out_shape=jax.ShapeDtypeStruct((3, 3, 3, cin, cout), jnp.float32),
        scratch_shapes=[pltpu.VMEM((2, 2 * cin, frames * span), jnp.bfloat16)],
        compiler_params=pltpu.CompilerParams(vmem_limit_bytes=LIMIT),
        cost_estimate=flops(work, 20 << 20),
        name="weight_grad",
    )(feat, shifts)
    back = back.transpose(1, 2, 0, 3).reshape(3, tokens_here, inner)
    return (weight_grad, back)


def solution(mesh):
    placed = (
        P("group", "seq", None, None),
        P("group", "seq", None, None),
        P(),
        P("seq", None),
        P(None, ("group", "seq"), None),
    )
    return jax.shard_map(
        per_device,
        mesh=mesh,
        in_specs=placed,
        out_specs=(P("group", None, None, None, None), P(None, ("group", "seq"), None)),
        check_vma=False,
    )
```

time: 615 us -> 262 us (0.43)
  waiting for transfers between devices: 392 us -> 63.9 us
  matrix products: 84.4 us -> 0 us
  Pallas kernels: 0 us -> 76.6 us
  blocking collectives: 0 us -> 25.6 us
  local copies, waits for them, and re-layouts: 64.1 us -> 49.5 us
  starting transfers between devices: 22.8 us -> 10.2 us
  other arithmetic: 29.3 us -> 20.7 us
    psum x1 -> x0, waiting for transfers between devices: 176 us -> none  [per_device(): lax.psum(local_grad, 'seq')]
    all_gather x1 -> x3, waiting for transfers between devices: 185 us -> 31 us  [the longest x1 24.1 us: per_device(): columns = lax.all_gather(piece, 'group', axis=0, tiled=False)]
    dot_general x95 -> x0, matrix products: 84.4 us -> none  [the longest x27 27.2 us: per_device(): lax.dot_general(flat_in, shifted, (((0,), (0,)), ((), ())), preferred_ele...]
    pallas_call x0 -> x3, Pallas kernels: none -> 76.6 us  [the longest x1 30.5 us: per_device(): pl.pallas_call(grad_out_kernel, grid=(blocks, 3), in_specs=[x_block, pl.B...]
    all_to_all x0 -> x1, blocking collectives: none -> 25.6 us  [per_device(): lax.all_to_all(piece.transpose(1, 0, 2), 'seq', split_axis=0, concat_axis...]
    unnamed x11 -> x8, local copies, waits for them, and re-layouts: 4.66 us -> 26.8 us
    squeeze x17 -> x1, local copies, waits for them, and re-layouts: 20.2 us -> 0.2 us  [per_device(): above = jnp.pad(wide[1][:, :-1], ((0, 0), (1, 0), (0, 0), (0, 0)))]
    concatenate x1 -> x2, other arithmetic: 1.02 us -> 15 us  [the longest x1 12.9 us: per_device(): jnp.concatenate([jnp.concatenate([taps[2], taps[1], taps[0], blank], axis...]
  transfers between devices with their start and end apart: 7 -> 5, of which waited for: 3 -> 4; matrix products, arithmetic and copies ran while one was open for 28% -> 23% of each run, Pallas kernels for 0% -> 29%
where the time goes in v1:
time: 262 us; the launch traced here: 261 us
  Pallas kernels  76.6 us (29%)
  waiting for transfers between devices  63.9 us (24%)
  local copies, waits for them, and re-layouts  49.5 us (19%)
  blocking collectives  25.6 us (10%)
  other arithmetic  20.7 us (8%)
  between operations  13.9 us (5%)
  starting transfers between devices  10.2 us (4%)
    all_to_all x1, waiting for transfers between devices, per_device(): lax.all_to_all(result, 'seq', split_axis=0, concat_axis=0, tiled=True)  32.9 us
    pallas_call x1, Pallas kernels, per_device(): pl.pallas_call(grad_out_kernel, grid=(blocks, 3), in_specs=[x_block, pl.B...  30.5 us
    unnamed x8, local copies, waits for them, and re-layouts  26.8 us
    all_to_all x1, blocking collectives, per_device(): lax.all_to_all(piece.transpose(1, 0, 2), 'seq', split_axis=0, concat_axis...  25.6 us
    pallas_call x1, Pallas kernels, per_device(): pl.pallas_call(lambda *refs: weight_kernel(scale, blocks, *refs), grid=(3...  24.6 us
    all_gather x1, waiting for transfers between devices, per_device(): columns = lax.all_gather(piece, 'group', axis=0, tiled=False)  24.1 us
    pallas_call x1, Pallas kernels, per_device(): pl.pallas_call(lambda *refs: attention_kernel(step, *refs), grid=(heads_h...  21.5 us
    concatenate x1, other arithmetic, per_device(): jnp.concatenate([jnp.concatenate([taps[2], taps[1], taps[0], blank], axis...  12.9 us
  transfers between devices with their start and end apart: 5, of which 4 were waited for; matrix products, arithmetic and copies ran while one was open for 23% of the time, Pallas kernels for 29%

profile of v1, /device:TPU:0, one launch (start us, length us, event | category | flops | bytes accessed | tf_op | source)
XLA Modules:
  0.0 260.5 jit_solution(7976161376421041125)
XLA Ops:
  9.1 2.8 %reshape.55 = bf16[192,8,4,128]{3,2,1,0:T(4,128)(2,1)S(1)} reshape(bf16[192,4096]{1,0:T(8,128)(2,1)} %param.8) | data formatting | bytes 3145728 | tf_op jit(solution)/shard_map/reshape | solution.py:172
  13.0 25.6 %all_to_all.15 = bf16[8,192,128]{2,1,0:T(8,128)(2,1)} all-to-all(bf16[8,192,128]{2,1,0:T(8,128)(2,1)S(1)} %bitcast.59), channel_id=1, replica_groups=mesh['group'=4,'seq'=8] {'seq'}, dimensions={0} | all-to-all | bytes 786432 | tf_op jit(solution)/shard_map/all_to_all | solution.py:174
  38.6 3.5 %copy.42 = bf16[3,128,4096]{1,2,0:T(8,128)(2,1)S(1)} copy(bf16[3,128,4096]{2,1,0:T(8,128)(2,1)} %param.9) | data formatting | bytes 6291456 | tf_op args[4]
  42.1 2.8 %copy.43 = bf16[3,128,8,512]{3,1,0,2:T(8,128)(2,1)} copy(bf16[3,128,8,512]{1,3,2,0:T(8,128)(2,1)S(1)} %bitcast.51) | data formatting | bytes 6291456 | tf_op jit(solution)/shard_map/reshape | solution.py:166
  44.8 4.6 %all-to-all-start = ((bf16[8,3,128,512]{3,2,1,0:T(8,128)(2,1)}), bf16[8,3,128,512]{3,2,1,0:T(8,128)(2,1)}, u32[]{:S(2)}, u32[]{:S(2)}) async-start(bf16[8,3,128,512]{3,2,1,0:T(8,128)(2,1)} %bitcast.16), calls=%async_computation | async-start | bytes 6291456 | tf_op jit(solution)/shard_map/all_to_all | solution.py:167
  50.4 4.1 %fusion = (bf16[3,3,1,384,192]{3,4,2,1,0:T(8,128)(2,1)S(1)}, bf16[3,3,1,384,192]{3,4,2,1,0:T(8,128)(2,1)}, bf16[3,3,1,384,192]{3,4,2,1,0:T(8,128)(2,1)}) fusion(bf16[3,3,3,384,192]{3,4,2,1,0:T(8,128)(2,1)} %param.7), kind=kLoop, calls=%fused_computation.12 | loop fusion | bytes 7962624 | tf_op jit(solution)/shard_map/slice | solution.py:193
  55.5 2.5 copy.54
  58.0 3.6 %copy.55 = bf16[3,3,1,384,192]{4,3,1,0,2:T(8,128)(2,1)} copy(bf16[3,3,1,384,192]{3,4,2,1,0:T(8,128)(2,1)} %get-tuple-element.16) | data formatting | bytes 2654208
  61.8 12.9 %maximum_maximum_fusion.w_ref = bf16[3,3,768,768]{3,2,1,0:T(8,128)(2,1)} fusion(bf16[3,3,384,192]{3,2,1,0:T(8,128)(2,1)} %bitcast.54, bf16[3,3,384,192]{3,2,1,0:T(8,128)(2,1)S(1)} %bitcast.53, bf16[3,3,384,192]{3,2,1,0:T(8,128)(2,1)S(1)} %bitcast.52, bf16[3,3,384,192]{3,2,1,0:T(8,128)(2,1)S(1)} %broadcast_in_dim.3), kind=kLoop, calls=%fused_computation | loop fusion | flops 84934656 | bytes 15925248 | tf_op jit(solution)/shard_map/concatenate | solution.py:195
  74.7 4.9 %all-gather.6.cloned.1.call-done = bf16[2048,384]{1,0:T(8,128)(2,1)} async-done(((bf16[256,384]{1,0:T(8,128)(2,1)}), bf16[2048,384]{1,0:T(8,128)(2,1)}) %all-gather.6.cloned.1.call-update) | async-done | bytes 1572880 | tf_op jit(solution)/shard_map/all_gather | solution.py:165
  79.6 1.6 copy.40
  82.6 2.0 pad_maximum_fusion.1
  85.3 5.8 %pad_maximum_fusion.x_ref.refs_1_ = bf16[4,4,256,768]{3,2,1,0:T(8,128)(2,1)} fusion(bf16[1,4,256,768]{3,2,1,0:T(8,128)(2,1)S(1)} %pad_bitcast_fusion, bf16[2,4,256,192]{3,2,1,0:T(8,128)(2,1)S(1)} %get-tuple-element.23, bf16[2,4,256,384]{3,2,1,0:T(8,128)(2,1)S(1)} %bitcast.48, bf16[2,4,256,192]{3,2,1,0:T(8,128)(2,1)S(1)} %get-tuple-element.26, ...), kind=kLoop, calls=%fused_computation.1 | loop fusion | flops 31457280 | bytes 12582912 | tf_op jit(solution)/shard_map/stack | solution.py:190
  91.1 24.1 %all-gather.8.cloned.1.call-done = bf16[4,1536,128]{2,1,0:T(8,128)(2,1)} async-done(((bf16[1,1536,128]{2,1,0:T(8,128)(2,1)}), bf16[4,1536,128]{2,1,0:T(8,128)(2,1)}) %all-gather.8.cloned.1.call-update) | async-done | bytes 1572880 | tf_op jit(solution)/shard_map/all_gather | solution.py:177
  115.2 2.7 %copy_bitcast_fusion.map_ref = bf16[1536,512]{1,0:T(8,128)(2,1)} fusion(bf16[4,1536,128]{2,1,0:T(8,128)(2,1)} %all-gather.8.cloned.1.call-done), kind=kLoop, calls=%fused_computation.3 | loop fusion | bytes 3145728 | tf_op jit(solution)/shard_map/reshape | solution.py:178
  118.0 30.5 %grad_out.1.refs_1_ = bf16[1024,512]{1,0:T(8,128)(2,1)} custom-call(bf16[4,4,256,768]{3,2,1,0:T(8,128)(2,1)} %pad_maximum_fusion.x_ref.refs_1_, bf16[3,3,768,768]{3,2,1,0:T(8,128)(2,1)} %maximum_maximum_fusion.w_ref, bf16[1536,512]{1,0:T(8,128)(2,1)} %copy_bitcast_fusion.map_ref), custom_call_target="tpu_custom_call" | custom-call | flops 16307453952 | bytes 20971520 | tf_op jit(solution)/shard_map/grad_out/pallas_call | solution.py:207
  148.4 21.5 %attention.1 = bf16[8,3,128,512]{3,2,1,0:T(8,128)(2,1)} custom-call(bf16[8,3,128,512]{3,2,1,0:T(8,128)(2,1)} %all-to-all-done.refs_0_, bf16[1024,512]{1,0:T(8,128)(2,1)} %grad_out.1.refs_1_), custom_call_target="tpu_custom_call" | custom-call | flops 10737418240 | bytes 8388608 | tf_op jit(solution)/shard_map/attention/pallas_call | solution.py:226
  170.0 5.5 %all-to-all-start.2 = ((bf16[8,3,128,512]{3,2,1,0:T(8,128)(2,1)}), bf16[8,3,128,512]{3,2,1,0:T(8,128)(2,1)S(1)}, u32[]{:S(2)}, u32[]{:S(2)}) async-start(bf16[8,3,128,512]{3,2,1,0:T(8,128)(2,1)} %attention.1), calls=%async_computation.2 | async-start | bytes 6291456 | tf_op jit(solution)/shard_map/all_to_all | solution.py:239
  175.5 2.0 all-gather.4.cloned.1.call-done
  177.5 24.6 %weight_grad.1 = f32[3,3,3,384,192]{4,3,2,1,0:T(8,128)} custom-call(bf16[8,2,4,32,768]{4,3,2,1,0:T(8,128)(2,1)} %bitcast.62, bf16[4,4,256,768]{3,2,1,0:T(8,128)(2,1)} %pad_maximum_fusion.x_ref.refs_1_), custom_call_target="tpu_custom_call" | custom-call | flops 16307453952 | bytes 20971520 | tf_op jit(solution)/shard_map/weight_grad/pallas_call | solution.py:243
  202.0 11.6 %copy.50 = f32[3,3,3,384,192]{3,4,2,1,0:T(8,128)} copy(f32[3,3,3,384,192]{4,3,2,1,0:T(8,128)} %weight_grad.1) | data formatting | bytes 15925248
  213.7 32.9 %all-to-all-done.2 = bf16[8,3,128,512]{3,2,1,0:T(8,128)(2,1)S(1)} async-done(((bf16[8,3,128,512]{3,2,1,0:T(8,128)(2,1)}), bf16[8,3,128,512]{3,2,1,0:T(8,128)(2,1)S(1)}, u32[]{:S(2)}, u32[]{:S(2)}) %all-to-all-start.2) | async-done | bytes 3145760 | tf_op jit(solution)/shard_map/all_to_all | solution.py:239
  246.6 2.8 %copy.49 = bf16[3,128,8,512]{1,3,2,0:T(8,128)(2,1)} copy(bf16[3,128,8,512]{3,1,0,2:T(8,128)(2,1)S(1)} %bitcast.49) | data formatting | bytes 6291456 | tf_op jit(solution)/shard_map/transpose | solution.py:259
  249.4 4.6 %copy.51 = bf16[3,128,4096]{2,1,0:T(8,128)(2,1)} copy(bf16[3,128,4096]{1,2,0:T(8,128)(2,1)} %bitcast.50) | data formatting | bytes 6291456
  (24 shorter events, 7.0 us)
Async XLA Ops:
  7.2 72.4 %all-gather.6.cloned.1.call-start = ((), (), s32[]{:S(2)}) async-start(), calls=%async_computation.4 | async-start | bytes 1769472 | tf_op jit(solution)/shard_map/all_gather | solution.py:165
  9.1 106.1 %all-gather.8.cloned.1.call-start = ((), (), s32[]{:S(2)}) async-start(), calls=%async_computation.5 | async-start | bytes 1966080 | tf_op jit(solution)/shard_map/all_gather | solution.py:177
  44.8 4.7 %copy-start = (bf16[4,8,16,384]{3,2,1,0:T(8,128)(2,1)S(1)}, bf16[4,8,16,384]{3,2,1,0:T(8,128)(2,1)}, u32[]{:S(2)}) copy-start(bf16[4,8,16,384]{3,2,1,0:T(8,128)(2,1)} %param.5) | copy-start | bytes 1179652
  44.8 103.6 %all-to-all-start = ((bf16[8,3,128,512]{3,2,1,0:T(8,128)(2,1)}), bf16[8,3,128,512]{3,2,1,0:T(8,128)(2,1)}, u32[]{:S(2)}, u32[]{:S(2)}) async-start(bf16[8,3,128,512]{3,2,1,0:T(8,128)(2,1)} %bitcast.16), calls=%async_computation | async-start | bytes 6291456 | tf_op jit(solution)/shard_map/all_to_all | solution.py:167
  49.4 128.0 %all-gather.4.cloned.1.call-start = ((), (), s32[]{:S(2)}) async-start(), calls=%async_computation.3 | async-start | bytes 3538944 | tf_op jit(solution)/shard_map/all_gather | solution.py:180
  170.0 76.6 %all-to-all-start.2 = ((bf16[8,3,128,512]{3,2,1,0:T(8,128)(2,1)}), bf16[8,3,128,512]{3,2,1,0:T(8,128)(2,1)S(1)}, u32[]{:S(2)}, u32[]{:S(2)}) async-start(bf16[8,3,128,512]{3,2,1,0:T(8,128)(2,1)} %attention.1), calls=%async_computation.2 | async-start | bytes 6291456 | tf_op jit(solution)/shard_map/all_to_all | solution.py:239
Sparse Core Ops, SparseCore 0:
  10.2 69.3 all-gather.5
  81.1 34.0 all-gather.7
  117.4 60.0 all-gather.3
